TPU v7x, 32 devices: a whole 2x2x4 slice. The times are simulated.
32 devices in a mesh: grp: 2 (over x), row: 8 (over z, y), col: 2 (over core).
Axes of the slice: x: 2, y: 2, z: 4, core: 2. Of those that a mesh axis runs over, the one named last changes fastest.
Arguments:
- upstream: float32 [1024, 384, 256], P(('grp', 'row'), 'col'), parts along dimension 0, may hold values from -6 to 6
- angle_codes: int32 [6, 2], P('grp'), parts along dimension 0, may hold values from 0 to 359
Outputs:
- downstream: float32 [1024, 384, 256], P('grp', 'row', 'col'), parts along dimension 0
There are 2 independent parts, one for each index of `grp`. A program takes and returns all parts, laid end to end along the dimension named above; each array names one. Nothing has to cross between parts.
All inputs are finite; a program needn't handle non-finite values.
Results may differ from a plain program's by a relative error of at most 0.0003.
Values sent between devices are 32-bit elements; how exact they have to be, the bound alone decides.
No kernel may reach another device: no remote copies, remote signals or barrier semaphores. Data moves between devices by JAX's collectives and lax.ppermute only.
A program may use at most 128 MiB of HBM per device.

v0:
```python
import math
import jax
import jax.numpy as jnp
from jax import lax
from jax.sharding import PartitionSpec as P

ANGLES = 360
TWO_PI = 2.0 * math.pi
einsum_forms = ("akl,am->mkl", "kal,am->kml", "kla,am->klm")


def shear_factors_of(angle_codes):
    return jnp.tan((angle_codes.astype(jnp.float32) - ANGLES / 2) * (math.pi / (2 * ANGLES)))


def centred(length, start, total):
    return (lax.iota(jnp.int32, length) + start).astype(jnp.float32) - total / 2


def contract(volume, matrix, along):
    return jnp.einsum(einsum_forms[along], volume, matrix, precision=lax.Precision.HIGHEST)


def shear_back(volume, along, offsets):
    length = volume.shape[along]
    position = lax.iota(jnp.int32, length)
    product = position[:, None] * position[None, :] % length
    angles_grid = product.astype(jnp.float32) * (TWO_PI / length)
    cosines = jnp.cos(angles_grid)
    sines = jnp.sin(angles_grid)
    frequency = jnp.where(position < length // 2, position, position - length).astype(jnp.float32)
    layout = [1, 1, 1]
    layout[along] = length
    phases = frequency.reshape(layout) * offsets * (TWO_PI / length)
    ramp_real = jnp.cos(phases)
    ramp_imag = jnp.sin(phases)
    spectrum_real = contract(volume, cosines, along)
    spectrum_imag = -contract(volume, sines, along)
    turned_real = spectrum_real * ramp_real - spectrum_imag * ramp_imag
    turned_imag = spectrum_real * ramp_imag + spectrum_imag * ramp_real
    return (contract(turned_real, cosines, along) - contract(turned_imag, sines, along)) / length


def body(upstream, angle_codes):
    factors = shear_factors_of(angle_codes)
    row_count = lax.axis_size("row")
    col_count = lax.axis_size("col")
    row_place = lax.axis_index("row")
    col_place = lax.axis_index("col")
    first_local, second_local, third_full = upstream.shape
    first_full = first_local * row_count
    second_full = second_local * col_count
    first_coords = centred(first_local, row_place * first_local, first_full)
    second_coords = centred(second_local, col_place * second_local, second_full)
    offsets = (
        factors[2, 0] * first_coords[:, None, None] + factors[2, 1] * second_coords[None, :, None]
    )
    turned = shear_back(upstream, 2, offsets)
    third_local = third_full // col_count
    second_part = second_full // row_count
    slab_volume = lax.all_to_all(turned, "col", split_axis=0, concat_axis=1, tiled=True)
    slab_width = first_local // col_count
    slab_coords = centred(slab_width, (row_place * col_count + col_place) * slab_width, first_full)
    whole_third = centred(third_full, 0, third_full)
    offsets = (
        factors[1, 0] * slab_coords[:, None, None] + factors[1, 1] * whole_third[None, None, :]
    )
    turned = shear_back(slab_volume, 1, offsets)
    arrived = lax.all_to_all(
        lax.all_to_all(turned, "row", split_axis=1, concat_axis=0, tiled=True),
        "col",
        split_axis=2,
        concat_axis=0,
        tiled=True,
    )
    arrived = arrived.reshape(col_count, row_count, slab_width, second_part, third_local)
    arrived = arrived.transpose(1, 0, 2, 3, 4).reshape(first_full, second_part, third_local)
    out_second = centred(second_part, row_place * second_part, second_full)
    out_third = centred(third_local, col_place * third_local, third_full)
    offsets = factors[0, 0] * out_second[None, :, None] + factors[0, 1] * out_third[None, None, :]
    return shear_back(arrived, 0, offsets)


def solution(mesh):
    placed = (P(("grp", "row"), "col", None), P("grp", None))
    return jax.shard_map(
        body, mesh=mesh, in_specs=placed, out_specs=P("grp", "row", "col"), check_vma=False
    )
```

profile of v0, /device:TPU:0, one launch (start us, length us, event | category | flops | bytes accessed | tf_op | source)
XLA Modules:
  0.0 1031.7 jit_solution(5909526161043933618)
XLA Ops:
  0.0 0.0 copy-start.5
  0.0 17.7 %fusion.119 = f32[256,64,192]{0,2,1:T(8,128)} fusion(f32[64,192,256]{2,1,0:T(8,128)} %param.2), kind=kOutput, calls=%fused_computation.107 | convolution fusion | flops 9664593920 | bytes 25165824 | tf_op jit(solution)/shard_map/kla,am->klm/dot_general | solution.py:21
  17.7 0.0 copy-done.5
  17.7 15.3 %fusion.122 = f32[256,64,192]{0,2,1:T(8,128)} fusion(f32[64,192,256]{2,1,0:T(8,128)S(1)} %copy-done.5), kind=kOutput, calls=%fused_computation.110 | convolution fusion | flops 9664593920 | bytes 25165824 | tf_op jit(solution)/shard_map/kla,am->klm/dot_general | solution.py:21
  33.0 1.0 fusion.225
  34.0 1.0 fusion.233
  35.0 0.0 copy-done.6
  35.0 0.6 fusion.180
  35.7 0.6 add_multiply_fusion.1
  36.3 0.6 add_multiply_fusion.5
  36.9 0.1 broadcast_add_fusion
  37.0 0.0 copy-start.4
  37.0 84.5 %fusion.7 = f32[64,192,256]{2,1,0:T(8,128)S(1)} fusion(f32[256,64,192]{0,2,1:T(8,128)} %fusion.122, f32[256,64,192]{0,2,1:T(8,128)} %fusion.119, f32[64,192]{1,0:T(8,128)S(1)} %broadcast_add_fusion, f32[256]{0:T(256)S(1)} %fusion.135, f32[256,256,1]{1,0,2:T(8,128)S(1)} %fusion.225), kind=kOutput, calls=%fused_computation.11 | convolution fusion | flops 9682550784 | bytes 38061056 | tf_op jit(solution)/shard_map/kla,am->klm/dot_general | solution.py:21
  121.6 0.0 copy-done.3
  121.6 0.0 copy-done.4
  121.6 59.0 %subtract_multiply_fusion.1 = f32[64,192,256]{2,1,0:T(8,128)S(1)} fusion(f32[64,192,256]{2,1,0:T(8,128)S(1)} %fusion.7, f32[256,64,192]{0,2,1:T(8,128)S(1)} %copy-done.4, f32[256,64,192]{0,2,1:T(8,128)S(1)} %copy-done.3, f32[64,192]{1,0:T(8,128)S(1)} %broadcast_add_fusion, f32[256]{0:T(256)S(1)} %fusion.135, f32[256,256,1]{1,0,2:T(8,128)S(1)} %fusion.233), kind=kOutput, calls=%fused_computation.32 | convolution fusion | flops 9688842240 | bytes 50643968 | tf_op jit(solution)/shard_map/kla,am->klm/dot_general | solution.py:21
  180.6 15.7 %all_to_all.51 = f32[64,192,256]{2,1,0:T(8,128)} all-to-all(f32[64,192,256]{2,1,0:T(8,128)S(1)} %subtract_multiply_fusion.1), channel_id=1, replica_groups=mesh['grp'=2,'row'=8,'col'=2] {'col'}, dimensions={0} | all-to-all | bytes 25165824 | tf_op jit(solution)/shard_map/all_to_all | solution.py:61
  196.2 10.8 %copy.24 = f32[32,2,192,256]{3,2,1,0:T(8,128)} copy(f32[32,2,192,256]{3,2,0,1:T(8,128)} %bitcast.163) | data formatting | bytes 25165824 | tf_op jit(solution)/shard_map/all_to_all | solution.py:61
  207.1 33.1 %fusion.83 = f32[384,32,256]{2,0,1:T(8,128)} fusion(f32[32,384,256]{2,1,0:T(8,128)} %bitcast.159), kind=kOutput, calls=%fused_computation.79 | convolution fusion | flops 14496841728 | bytes 25165824 | tf_op jit(solution)/shard_map/kal,am->kml/dot_general | solution.py:21
  240.2 0.0 copy-done
  240.2 31.4 %fusion.86 = f32[384,32,256]{2,0,1:T(8,128)} fusion(f32[32,384,256]{2,1,0:T(8,128)S(1)} %bitcast.160), kind=kOutput, calls=%fused_computation.82 | convolution fusion | flops 14496841728 | bytes 25165824 | tf_op jit(solution)/shard_map/kal,am->kml/dot_general | solution.py:21
  271.6 2.2 fusion.223
  273.9 2.2 fusion.231
  276.1 0.6 add_multiply_fusion
  276.7 0.6 add_multiply_fusion.4
  277.3 0.1 broadcast_add_fusion.1
  277.4 70.4 %fusion.1 = f32[384,32,256]{2,0,1:T(8,128)S(1)} fusion(f32[384,32,256]{2,0,1:T(8,128)} %fusion.86, f32[384,32,256]{2,0,1:T(8,128)} %fusion.83, f32[32,256]{1,0:T(8,128)S(1)} %broadcast_add_fusion.1, f32[384]{0:T(512)S(1)} %fusion.133, f32[384,384,1]{0,1,2:T(8,128)S(1)} %fusion.223), kind=kOutput, calls=%fused_computation.3 | convolution fusion | flops 14514388992 | bytes 38372864 | tf_op jit(solution)/shard_map/kal,am->kml/dot_general | solution.py:21
  347.8 72.5 %multiply_bitcast_fusion = f32[32,384,256]{2,1,0:T(8,128)} fusion(f32[384,32,256]{2,0,1:T(8,128)S(1)} %fusion.1, f32[384,32,256]{2,0,1:T(8,128)} %fusion.86, f32[384,32,256]{2,0,1:T(8,128)} %fusion.83, f32[32,256]{1,0:T(8,128)S(1)} %broadcast_add_fusion.1, f32[384]{0:T(512)S(1)} %fusion.133, f32[384,384,1]{0,1,2:T(8,128)S(1)} %fusion.231), kind=kOutput, calls=%fused_computation.28 | convolution fusion | flops 14520680448 | bytes 50955776 | tf_op jit(solution)/shard_map/kal,am->kml/dot_general | solution.py:21
  420.4 16.6 %copy.25 = f32[32,384,256]{2,0,1:T(8,128)} copy(f32[32,384,256]{2,1,0:T(8,128)} %multiply_bitcast_fusion) | data formatting | bytes 25165824 | tf_op jit(solution)/shard_map/div | solution.py:41
  437.0 7.4 all-to-all-start.1
  444.4 0.6 add_multiply_fusion.3
  445.1 0.7 add_multiply_fusion.2
  445.8 3.8 fusion.229
  449.6 3.8 fusion.227
  453.4 0.1 broadcast_add_fusion.2
  453.5 264.2 %all-to-all-done.1 = f32[32,384,256]{2,0,1:T(8,128)} async-done(((f32[32,384,256]{2,0,1:T(8,128)}), f32[32,384,256]{2,0,1:T(8,128)}, u32[]{:S(2)}, u32[]{:S(2)}) %all-to-all-start.1) | async-done | bytes 12582944 | tf_op jit(solution)/shard_map/all_to_all | solution.py:70
  717.6 16.8 %copy.27 = f32[8,32,48,256]{3,2,1,0:T(8,128)} copy(f32[8,32,48,256]{3,1,2,0:T(8,128)} %bitcast.19) | data formatting | bytes 25165824 | tf_op jit(solution)/shard_map/all_to_all | solution.py:70
  734.4 12.9 %copy.28 = f32[256,48,256]{0,1,2:T(8,128)} copy(f32[256,48,256]{2,1,0:T(8,128)} %bitcast.164) | data formatting | bytes 25165824 | tf_op jit(solution)/shard_map/all_to_all | solution.py:70
  747.3 25.0 %all_to_all.52 = f32[256,48,256]{0,1,2:T(8,128)} all-to-all(f32[256,48,256]{0,1,2:T(8,128)} %copy.28), channel_id=1, replica_groups=mesh['grp'=2,'row'=8,'col'=2] {'col'}, dimensions={2} | all-to-all | bytes 25165824 | tf_op jit(solution)/shard_map/all_to_all | solution.py:69
  772.3 12.8 %copy.30 = f32[2,256,48,128]{3,2,1,0:T(8,128)} copy(f32[2,256,48,128]{1,2,3,0:T(8,128)} %bitcast.165) | data formatting | bytes 25165824 | tf_op jit(solution)/shard_map/all_to_all | solution.py:69
  785.1 13.1 %copy.31 = f32[8,2,32,48,128]{4,2,1,0,3:T(8,128)} copy(f32[8,2,32,48,128]{4,3,2,0,1:T(8,128)} %bitcast.166) | data formatting | bytes 25165824 | tf_op jit(solution)/shard_map/transpose | solution.py:77
  798.2 36.5 %fusion.72 = f32[512,48,128]{2,0,1:T(8,128)S(1)} fusion(f32[512,48,128]{2,0,1:T(8,128)} %bitcast.161), kind=kOutput, calls=%fused_computation.67 | convolution fusion | flops 19331022848 | bytes 25165824 | tf_op jit(solution)/shard_map/akl,am->mkl/dot_general | solution.py:21
  834.7 0.0 copy-done.1
  834.7 34.1 %fusion.75 = f32[512,48,128]{2,0,1:T(8,128)} fusion(f32[512,48,128]{2,0,1:T(8,128)S(1)} %bitcast.162), kind=kOutput, calls=%fused_computation.70 | convolution fusion | flops 19331022848 | bytes 25165824 | tf_op jit(solution)/shard_map/akl,am->mkl/dot_general | solution.py:21
  868.9 72.7 %fusion.12 = f32[512,48,128]{2,0,1:T(8,128)} fusion(f32[512,48,128]{2,0,1:T(8,128)} %fusion.75, f32[512,48,128]{2,0,1:T(8,128)S(1)} %fusion.72, f32[48,128]{1,0:T(8,128)S(1)} %broadcast_add_fusion.2, f32[512]{0:T(512)S(1)} %fusion.134, f32[512,512,1]{0,1,2:T(8,128)S(1)} %fusion.229), kind=kOutput, calls=%fused_computation.17 | convolution fusion | flops 19346227200 | bytes 38823936 | tf_op jit(solution)/shard_map/akl,am->mkl/dot_general | solution.py:21
  941.6 0.0 copy-done.2
  941.6 73.0 %subtract_multiply_fusion = f32[512,48,128]{2,0,1:T(8,128)} fusion(f32[512,48,128]{2,0,1:T(8,128)} %fusion.12, f32[512,48,128]{2,0,1:T(8,128)S(1)} %copy-done.2, f32[512,48,128]{2,0,1:T(8,128)S(1)} %fusion.72, f32[48,128]{1,0:T(8,128)S(1)} %broadcast_add_fusion.2, f32[512]{0:T(512)S(1)} %fusion.134, f32[512,512,1]{0,1,2:T(8,128)S(1)} %fusion.227), kind=kOutput, calls=%fused_computation.16 | convolution fusion | flops 19352518656 | bytes 51406848 | tf_op jit(solution)/shard_map/akl,am->mkl/dot_general | solution.py:21
  1014.6 16.6 %copy.32 = f32[512,48,128]{2,1,0:T(8,128)} copy(f32[512,48,128]{2,0,1:T(8,128)} %subtract_multiply_fusion) | data formatting | bytes 25165824 | tf_op jit(solution)/shard_map/div | solution.py:41
  (9 shorter events, 0.1 us)
Async XLA Ops:
  0.0 17.7 %copy-start.5 = (f32[64,192,256]{2,1,0:T(8,128)S(1)}, f32[64,192,256]{2,1,0:T(8,128)}, u32[]{:S(2)}) copy-start(f32[64,192,256]{2,1,0:T(8,128)} %param.2) | copy-start | bytes 37748740
  17.7 17.2 %copy-start.6 = (s32[3,2]{0,1:T(2,128)S(1)}, s32[3,2]{0,1:T(2,128)}, u32[]{:S(2)}) copy-start(s32[3,2]{0,1:T(2,128)} %param.3) | copy-start | bytes 76
  37.0 84.6 %copy-start.3 = (f32[256,64,192]{0,2,1:T(8,128)S(1)}, f32[256,64,192]{0,2,1:T(8,128)}, u32[]{:S(2)}) copy-start(f32[256,64,192]{0,2,1:T(8,128)} %fusion.119) | copy-start | bytes 37748740
  37.0 84.6 %copy-start.4 = (f32[256,64,192]{0,2,1:T(8,128)S(1)}, f32[256,64,192]{0,2,1:T(8,128)}, u32[]{:S(2)}) copy-start(f32[256,64,192]{0,2,1:T(8,128)} %fusion.122) | copy-start | bytes 37748740
  207.1 33.1 %copy-start = (f32[32,2,192,256]{3,2,1,0:T(8,128)S(1)}, f32[32,2,192,256]{3,2,1,0:T(8,128)}, u32[]{:S(2)}) copy-start(f32[32,2,192,256]{3,2,1,0:T(8,128)} %copy.24) | copy-start | bytes 37748740
  437.0 280.6 %all-to-all-start.1 = ((f32[32,384,256]{2,0,1:T(8,128)}), f32[32,384,256]{2,0,1:T(8,128)}, u32[]{:S(2)}, u32[]{:S(2)}) async-start(f32[32,384,256]{2,0,1:T(8,128)} %copy.25), calls=%async_computation.1 | async-start | bytes 25165824 | tf_op jit(solution)/shard_map/all_to_all | solution.py:70
  798.2 36.5 %copy-start.1 = (f32[8,2,32,48,128]{4,2,1,0,3:T(8,128)S(1)}, f32[8,2,32,48,128]{4,2,1,0,3:T(8,128)}, u32[]{:S(2)}) copy-start(f32[8,2,32,48,128]{4,2,1,0,3:T(8,128)} %copy.31) | copy-start | bytes 37748740
  868.9 72.7 %copy-start.2 = (f32[512,48,128]{2,0,1:T(8,128)S(1)}, f32[512,48,128]{2,0,1:T(8,128)}, u32[]{:S(2)}) copy-start(f32[512,48,128]{2,0,1:T(8,128)} %fusion.75) | copy-start | bytes 37748740
where the time goes:
time: 1040 us; the launch traced here: 1030 us
  matrix products  600 us (58%)
  waiting for transfers between devices  264 us (25%)
  local copies, waits for them, and re-layouts  100 us (10%)
  blocking collectives  40.7 us (4%)
  other arithmetic  18 us (2%)
    dot_general x12, matrix products, contract(): jnp.einsum(einsum_forms[along], volume, matrix, precision=lax.Precision.H...  600 us
    all_to_all x1, waiting for transfers between devices, body(): lax.all_to_all(turned, 'row', split_axis=1, concat_axis=0, tiled=True)  264 us
    div x2, local copies, waits for them, and re-layouts, shear_back(): (contract(turned_real, cosines, along) - contract(turned_imag, sines, alo...  33.3 us
    all_to_all x2, local copies, waits for them, and re-layouts, body(): lax.all_to_all(turned, 'row', split_axis=1, concat_axis=0, tiled=True)  29.6 us
    all_to_all x1, blocking collectives, body(): lax.all_to_all(lax.all_to_all(turned, 'row', split_axis=1, concat_axis=0,...  25 us
  transfers between devices with their start and end apart: 1, of which 1 were waited for; matrix products, arithmetic and copies ran while one was open for 1% of the time, Pallas kernels for 0%

commit v1 on v0

--- a/solution.py
+++ b/solution.py
@@ -66,12 +66,20 @@
         factors[1, 0] * slab_coords[:, None, None] + factors[1, 1] * whole_third[None, None, :]
     )
     turned = shear_back(slab_volume, 1, offsets)
-    arrived = lax.all_to_all(
-        lax.all_to_all(turned, "row", split_axis=1, concat_axis=0, tiled=True),
-        "col",
-        split_axis=2,
-        concat_axis=0,
-        tiled=True,
+    arrived = jnp.concatenate(
+        lax.all_to_all(
+            jnp.stack(
+                jnp.split(
+                    lax.all_to_all(turned, "row", split_axis=1, concat_axis=0, tiled=True),
+                    lax.axis_size("col"),
+                    axis=2,
+                )
+            ),
+            "col",
+            0,
+            0,
+        ),
+        axis=0,
     )
     arrived = arrived.reshape(col_count, row_count, slab_width, second_part, third_local)
     arrived = arrived.transpose(1, 0, 2, 3, 4).reshape(first_full, second_part, third_local)

time: 1040 us -> 1030 us (level)
  local copies, waits for them, and re-layouts: 100 us -> 82.8 us
  other arithmetic: 18 us -> 28.6 us
    all_to_all x2 -> x1, local copies, waits for them, and re-layouts: 29.6 us -> 16.5 us  [body(): lax.all_to_all(turned, 'row', split_axis=1, concat_axis=0, tiled=True)]
    all_to_all x1 -> x0, local copies, waits for them, and re-layouts: 12.8 us -> none  [body(): lax.all_to_all(lax.all_to_all(turned, 'row', split_axis=1, concat_axis=0,...]
where the time goes in v1:
time: 1030 us; the launch traced here: 1020 us
  matrix products  600 us (58%)
  waiting for transfers between devices  263 us (26%)
  local copies, waits for them, and re-layouts  82.8 us (8%)
  blocking collectives  41.3 us (4%)
  other arithmetic  28.6 us (3%)
    dot_general x12, matrix products, contract(): jnp.einsum(einsum_forms[along], volume, matrix, precision=lax.Precision.H...  600 us
    all_to_all x1, waiting for transfers between devices, body(): lax.all_to_all(turned, 'row', split_axis=1, concat_axis=0, tiled=True)  263 us
    div x2, local copies, waits for them, and re-layouts, shear_back(): (contract(turned_real, cosines, along) - contract(turned_imag, sines, alo...  33.3 us
    all_to_all x1, blocking collectives, body(): lax.all_to_all(jnp.stack(jnp.split(lax.all_to_all(turned, 'row', split_ax...  25.5 us
  transfers between devices with their start and end apart: 1, of which 1 were waited for; matrix products, arithmetic and copies ran while one was open for 1% of the time, Pallas kernels for 0%

profile of v1, /device:TPU:0, one launch (start us, length us, event | category | flops | bytes accessed | tf_op | source)
XLA Modules:
  0.0 1023.7 jit_solution(3839630993687746718)
XLA Ops:
  0.0 17.7 %fusion.119 = f32[256,64,192]{0,2,1:T(8,128)} fusion(f32[64,192,256]{2,1,0:T(8,128)} %param.2), kind=kOutput, calls=%fused_computation.110 | convolution fusion | flops 9664593920 | bytes 25165824 | tf_op jit(solution)/shard_map/kla,am->klm/dot_general | solution.py:21
  17.7 0.0 copy-done.5
  17.7 15.3 %fusion.122 = f32[256,64,192]{0,2,1:T(8,128)} fusion(f32[64,192,256]{2,1,0:T(8,128)S(1)} %copy-done.5), kind=kOutput, calls=%fused_computation.113 | convolution fusion | flops 9664593920 | bytes 25165824 | tf_op jit(solution)/shard_map/kla,am->klm/dot_general | solution.py:21
  33.0 1.0 fusion.225
  34.0 1.0 fusion.233
  34.9 0.0 copy-done.8
  35.0 0.7 fusion.180
  35.7 0.6 add_multiply_fusion.1
  36.3 0.7 add_multiply_fusion.5
  37.0 0.1 broadcast_add_fusion
  37.1 0.0 copy-start.4
  37.1 84.6 %fusion.7 = f32[64,192,256]{2,1,0:T(8,128)S(1)} fusion(f32[256,64,192]{0,2,1:T(8,128)} %fusion.122, f32[256,64,192]{0,2,1:T(8,128)} %fusion.119, f32[64,192]{1,0:T(8,128)S(1)} %broadcast_add_fusion, f32[256]{0:T(256)S(1)} %fusion.135, f32[256,256,1]{1,0,2:T(8,128)S(1)} %fusion.225), kind=kOutput, calls=%fused_computation.12 | convolution fusion | flops 9682550784 | bytes 38061056 | tf_op jit(solution)/shard_map/kla,am->klm/dot_general | solution.py:21
  121.7 0.0 copy-done.3
  121.7 0.0 copy-done.4
  121.7 59.0 %subtract_multiply_fusion.1 = f32[64,192,256]{2,1,0:T(8,128)S(1)} fusion(f32[64,192,256]{2,1,0:T(8,128)S(1)} %fusion.7, f32[256,64,192]{0,2,1:T(8,128)S(1)} %copy-done.4, f32[256,64,192]{0,2,1:T(8,128)S(1)} %copy-done.3, f32[64,192]{1,0:T(8,128)S(1)} %broadcast_add_fusion, f32[256]{0:T(256)S(1)} %fusion.135, f32[256,256,1]{1,0,2:T(8,128)S(1)} %fusion.233), kind=kOutput, calls=%fused_computation.33 | convolution fusion | flops 9688842240 | bytes 50643968 | tf_op jit(solution)/shard_map/kla,am->klm/dot_general | solution.py:21
  180.7 15.9 %all_to_all.41 = f32[64,192,256]{2,1,0:T(8,128)} all-to-all(f32[64,192,256]{2,1,0:T(8,128)S(1)} %subtract_multiply_fusion.1), channel_id=1, replica_groups=mesh['grp'=2,'row'=8,'col'=2] {'col'}, dimensions={0} | all-to-all | bytes 25165824 | tf_op jit(solution)/shard_map/all_to_all | solution.py:61
  196.5 10.8 %copy.13 = f32[32,2,192,256]{3,2,1,0:T(8,128)} copy(f32[32,2,192,256]{3,2,0,1:T(8,128)} %bitcast.165) | data formatting | bytes 25165824 | tf_op jit(solution)/shard_map/all_to_all | solution.py:61
  207.4 33.1 %fusion.83 = f32[384,32,256]{2,0,1:T(8,128)} fusion(f32[32,384,256]{2,1,0:T(8,128)} %bitcast.160), kind=kOutput, calls=%fused_computation.82 | convolution fusion | flops 14496841728 | bytes 25165824 | tf_op jit(solution)/shard_map/kal,am->kml/dot_general | solution.py:21
  240.5 0.0 copy-done
  240.5 31.2 %fusion.86 = f32[384,32,256]{2,0,1:T(8,128)} fusion(f32[32,384,256]{2,1,0:T(8,128)S(1)} %bitcast.161), kind=kOutput, calls=%fused_computation.85 | convolution fusion | flops 14496841728 | bytes 25165824 | tf_op jit(solution)/shard_map/kal,am->kml/dot_general | solution.py:21
  271.7 2.2 fusion.223
  273.9 2.2 fusion.231
  276.2 0.6 add_multiply_fusion
  276.8 0.6 add_multiply_fusion.4
  277.4 0.1 broadcast_add_fusion.1
  277.5 70.5 %fusion.1 = f32[384,32,256]{2,0,1:T(8,128)S(1)} fusion(f32[384,32,256]{2,0,1:T(8,128)} %fusion.86, f32[384,32,256]{2,0,1:T(8,128)} %fusion.83, f32[32,256]{1,0:T(8,128)S(1)} %broadcast_add_fusion.1, f32[384]{0:T(512)S(1)} %fusion.133, f32[384,384,1]{0,1,2:T(8,128)S(1)} %fusion.223), kind=kOutput, calls=%fused_computation.4 | convolution fusion | flops 14514388992 | bytes 38372864 | tf_op jit(solution)/shard_map/kal,am->kml/dot_general | solution.py:21
  348.0 72.5 %multiply_bitcast_fusion = f32[32,384,256]{2,1,0:T(8,128)} fusion(f32[384,32,256]{2,0,1:T(8,128)S(1)} %fusion.1, f32[384,32,256]{2,0,1:T(8,128)} %fusion.86, f32[384,32,256]{2,0,1:T(8,128)} %fusion.83, f32[32,256]{1,0:T(8,128)S(1)} %broadcast_add_fusion.1, f32[384]{0:T(512)S(1)} %fusion.133, f32[384,384,1]{0,1,2:T(8,128)S(1)} %fusion.231), kind=kOutput, calls=%fused_computation.29 | convolution fusion | flops 14520680448 | bytes 50955776 | tf_op jit(solution)/shard_map/kal,am->kml/dot_general | solution.py:21
  420.5 16.6 %copy.14 = f32[32,384,256]{2,0,1:T(8,128)} copy(f32[32,384,256]{2,1,0:T(8,128)} %multiply_bitcast_fusion) | data formatting | bytes 25165824 | tf_op jit(solution)/shard_map/div | solution.py:41
  437.1 7.5 all-to-all-start.1
  444.7 0.6 add_multiply_fusion.3
  445.2 0.6 add_multiply_fusion.2
  445.8 4.6 fusion.229
  450.4 4.6 fusion.227
  455.0 0.1 broadcast_add_fusion.2
  455.1 262.9 %all-to-all-done.1 = f32[32,384,256]{2,0,1:T(8,128)} async-done(((f32[32,384,256]{2,0,1:T(8,128)}), f32[32,384,256]{2,0,1:T(8,128)}, u32[]{:S(2)}, u32[]{:S(2)}) %all-to-all-start.1) | async-done | bytes 12582944 | tf_op jit(solution)/shard_map/all_to_all | solution.py:73
  717.9 16.5 %copy.16 = f32[8,32,48,256]{3,2,1,0:T(8,128)} copy(f32[8,32,48,256]{3,1,2,0:T(8,128)} %bitcast.19) | data formatting | bytes 25165824 | tf_op jit(solution)/shard_map/all_to_all | solution.py:73
  734.5 8.1 slice_bitcast_fusion.1
  742.6 9.0 pad_maximum_fusion
  751.6 25.5 %all_to_all.42 = f32[2,256,48,128]{3,2,1,0:T(8,128)} all-to-all(f32[2,256,48,128]{3,2,1,0:T(8,128)} %pad_maximum_fusion), channel_id=1, replica_groups=mesh['grp'=2,'row'=8,'col'=2] {'col'}, dimensions={0} | all-to-all | bytes 25165824 | tf_op jit(solution)/shard_map/all_to_all | solution.py:70
  777.1 13.4 %copy.17 = f32[8,2,32,48,128]{4,2,1,0,3:T(8,128)} copy(f32[8,2,32,48,128]{4,3,2,0,1:T(8,128)} %bitcast.166) | data formatting | bytes 25165824 | tf_op jit(solution)/shard_map/transpose | solution.py:85
  790.5 36.2 %fusion.72 = f32[512,48,128]{2,0,1:T(8,128)S(1)} fusion(f32[512,48,128]{2,0,1:T(8,128)} %bitcast.162), kind=kOutput, calls=%fused_computation.70 | convolution fusion | flops 19331022848 | bytes 25165824 | tf_op jit(solution)/shard_map/akl,am->mkl/dot_general | solution.py:21
  826.7 0.0 copy-done.1
  826.7 0.0 copy-start.7
  826.7 34.1 %fusion.75 = f32[512,48,128]{2,0,1:T(8,128)} fusion(f32[512,48,128]{2,0,1:T(8,128)S(1)} %bitcast.163), kind=kOutput, calls=%fused_computation.73 | convolution fusion | flops 19331022848 | bytes 25165824 | tf_op jit(solution)/shard_map/akl,am->mkl/dot_general | solution.py:21
  860.8 0.0 copy-done.7
  860.9 72.7 %fusion.12 = f32[512,48,128]{2,0,1:T(8,128)} fusion(f32[512,48,128]{2,0,1:T(8,128)} %fusion.75, f32[512,48,128]{2,0,1:T(8,128)S(1)} %fusion.72, f32[48,128]{1,0:T(8,128)S(1)} %broadcast_add_fusion.2, f32[512]{0:T(512)S(1)} %fusion.134, f32[512,512,1]{0,1,2:T(8,128)S(1)} %copy-done.7), kind=kOutput, calls=%fused_computation.18 | convolution fusion | flops 19346227200 | bytes 38823936 | tf_op jit(solution)/shard_map/akl,am->mkl/dot_general | solution.py:21
  933.6 73.0 %subtract_multiply_fusion = f32[512,48,128]{2,0,1:T(8,128)} fusion(f32[512,48,128]{2,0,1:T(8,128)} %fusion.12, f32[512,48,128]{2,0,1:T(8,128)S(1)} %copy-done.2, f32[512,48,128]{2,0,1:T(8,128)S(1)} %fusion.72, f32[48,128]{1,0:T(8,128)S(1)} %broadcast_add_fusion.2, f32[512]{0:T(512)S(1)} %fusion.134, f32[512,512,1]{0,1,2:T(8,128)S(1)} %copy-done.6), kind=kOutput, calls=%fused_computation.17 | convolution fusion | flops 19352518656 | bytes 51406848 | tf_op jit(solution)/shard_map/akl,am->mkl/dot_general | solution.py:21
  1006.6 16.6 %copy.18 = f32[512,48,128]{2,1,0:T(8,128)} copy(f32[512,48,128]{2,0,1:T(8,128)} %subtract_multiply_fusion) | data formatting | bytes 25165824 | tf_op jit(solution)/shard_map/div | solution.py:41
  (13 shorter events, 0.1 us)
Async XLA Ops:
  0.0 17.7 %copy-start.5 = (f32[64,192,256]{2,1,0:T(8,128)S(1)}, f32[64,192,256]{2,1,0:T(8,128)}, u32[]{:S(2)}) copy-start(f32[64,192,256]{2,1,0:T(8,128)} %param.2) | copy-start | bytes 37748740
  17.7 17.2 %copy-start.8 = (s32[3,2]{0,1:T(2,128)S(1)}, s32[3,2]{0,1:T(2,128)}, u32[]{:S(2)}) copy-start(s32[3,2]{0,1:T(2,128)} %param.3) | copy-start | bytes 76
  37.1 84.6 %copy-start.3 = (f32[256,64,192]{0,2,1:T(8,128)S(1)}, f32[256,64,192]{0,2,1:T(8,128)}, u32[]{:S(2)}) copy-start(f32[256,64,192]{0,2,1:T(8,128)} %fusion.119) | copy-start | bytes 37748740
  37.1 84.6 %copy-start.4 = (f32[256,64,192]{0,2,1:T(8,128)S(1)}, f32[256,64,192]{0,2,1:T(8,128)}, u32[]{:S(2)}) copy-start(f32[256,64,192]{0,2,1:T(8,128)} %fusion.122) | copy-start | bytes 37748740
  207.4 33.1 %copy-start = (f32[32,2,192,256]{3,2,1,0:T(8,128)S(1)}, f32[32,2,192,256]{3,2,1,0:T(8,128)}, u32[]{:S(2)}) copy-start(f32[32,2,192,256]{3,2,1,0:T(8,128)} %copy.13) | copy-start | bytes 37748740
  437.1 280.8 %all-to-all-start.1 = ((f32[32,384,256]{2,0,1:T(8,128)}), f32[32,384,256]{2,0,1:T(8,128)}, u32[]{:S(2)}, u32[]{:S(2)}) async-start(f32[32,384,256]{2,0,1:T(8,128)} %copy.14), calls=%async_computation.1 | async-start | bytes 25165824 | tf_op jit(solution)/shard_map/all_to_all | solution.py:73
  790.5 36.2 %copy-start.1 = (f32[8,2,32,48,128]{4,2,1,0,3:T(8,128)S(1)}, f32[8,2,32,48,128]{4,2,1,0,3:T(8,128)}, u32[]{:S(2)}) copy-start(f32[8,2,32,48,128]{4,2,1,0,3:T(8,128)} %copy.17) | copy-start | bytes 37748740
  826.7 34.1 %copy-start.7 = (f32[512,512,1]{0,1,2:T(8,128)S(1)}, f32[512,512,1]{0,1,2:T(8,128)}, u32[]{:S(2)}) copy-start(f32[512,512,1]{0,1,2:T(8,128)} %fusion.229) | copy-start | bytes 3145732
  860.9 72.7 %copy-start.2 = (f32[512,48,128]{2,0,1:T(8,128)S(1)}, f32[512,48,128]{2,0,1:T(8,128)}, u32[]{:S(2)}) copy-start(f32[512,48,128]{2,0,1:T(8,128)} %fusion.75) | copy-start | bytes 37748740
  860.9 72.7 %copy-start.6 = (f32[512,512,1]{0,1,2:T(8,128)S(1)}, f32[512,512,1]{0,1,2:T(8,128)}, u32[]{:S(2)}) copy-start(f32[512,512,1]{0,1,2:T(8,128)} %fusion.227) | copy-start | bytes 3145732
